TPU v7x, 256 devices: a whole 4x4x8 slice. The times are simulated.
256 devices in a mesh: slab: 64 (over x_lo, y, z), subj: 2 (over core), tm: 2 (over x_hi).
Axes of the slice: x: 4 (x_hi: 2, x_lo: 2; x = x_hi * 2 + x_lo), y: 4, z: 8, core: 2. Of those that a mesh axis runs over, the one named last changes fastest.
Arguments:
- subject_data: bfloat16 [2, 128, 128, 2048], P('subj', 'slab', None, 'tm'), may hold values from -8 to 8
- template: bfloat16 [128, 128, 2048], P('slab', None, 'tm'), may hold values from -8 to 8
- neighbours: int32 [128, 27], P('slab'), may hold values from 0 to 127, as said below
- valid: int32 [128, 27], P('slab'), may hold values from 0 to 1, as said below
Outputs:
- new_template: bfloat16 [128, 128, 2048], P('slab', None, 'tm')
Inputs may be any that keep to these rules, and one draw needn't show every extreme that they name: `neighbours`: slots 9 l to 9 l + 8 of block b name blocks of the slab of b shifted by l - 1 (slabs hold 2 consecutive blocks); where that slab doesn't exist they name b itself. Slot 13 names b itself. `valid`: slot 13 is always 1; slots whose slab doesn't exist are 0.
All inputs are finite; a program needn't handle non-finite values.
Results may differ from a plain program's by a relative error of at most 0.007.
Values may be sent and summed in bfloat16 or wider, within the bound.
A program may use at most 64 MiB of HBM per device.

v0:
```python
import jax
import jax.numpy as jnp
from jax import lax
from jax.sharding import PartitionSpec as P

ITERS = 3


def from_everyone(x, axis):
    size = lax.axis_size(axis)
    return lax.all_to_all(jnp.broadcast_to(x[None], (size, *x.shape)), axis, 0, 0, tiled=True)


def over_copies(x, axis):
    everything = from_everyone(x, axis)
    return jnp.sum(everything, axis=0)


def laid_out(pieces, dim):
    pieces = jnp.moveaxis(pieces, 0, dim)
    lengths = pieces.shape
    return pieces.reshape(*lengths[:dim], lengths[dim] * lengths[dim + 1], *lengths[dim + 2 :])


def gather_directly(x, axis, dim):
    return laid_out(from_everyone(x, axis), dim)


def with_halo(cells, sides, width):
    for axis, dim in sides:
        count = lax.axis_size(axis)
        ends = count - 1
        head = lax.slice_in_dim(cells, 0, width, axis=dim)
        tail = lax.slice_in_dim(cells, cells.shape[dim] - width, cells.shape[dim], axis=dim)
        cells = jnp.concatenate(
            [
                lax.ppermute(tail, axis, [(i, (i + 1) % count) for i in range(ends)]),
                cells,
                lax.ppermute(head, axis, [((i + 1) % count, i) for i in range(ends)]),
            ],
            axis=dim,
        )
    return cells


def split_up(x, dim, size):
    before, after = (x.shape[:dim], x.shape[dim + 1 :])
    return jnp.moveaxis(x.reshape(*before, size, -1, *after), dim, 0)


def edges_of(length, count):
    unit = 8 if length >= 8 * count else 1
    return [length // unit * k // count * unit for k in range(1, count)]


def exchange_in_pieces(x, axis, pieces, split_dim, concat_dim):
    blocks = split_up(x, split_dim, lax.axis_size(axis))
    cut = max(range(1, max(2, blocks.ndim - 1)), key=lambda d: blocks.shape[d])
    gathered = []
    for piece in jnp.split(blocks, edges_of(blocks.shape[cut], pieces), axis=cut):
        if piece.size:
            gathered.append(lax.all_to_all(piece, axis, split_axis=0, concat_axis=0, tiled=True))
    return laid_out(jnp.concatenate(gathered, axis=cut), concat_dim)


def balance(cross, row_norm, col_norm, mask):
    width = cross.shape[-1]
    logits = cross * row_norm[None, :, None, None] * col_norm[:, None, :, :] / 0.03
    masked = mask[None, None, :, None]
    kernel = jnp.exp(logits) * masked
    target = masked / (width * jnp.sum(mask))
    filler = 1.0 - masked
    col_weight = jnp.ones((cross.shape[0], 1, cross.shape[2], width), jnp.float32)
    for step in range(ITERS):
        row_weight = 1.0 / width / jnp.sum(kernel * col_weight, axis=(2, 3), keepdims=True)
        col_weight = target / (jnp.sum(kernel * row_weight, axis=1, keepdims=True) + filler)
    flow = kernel * col_weight
    return (flow / jnp.sum(flow, axis=(2, 3), keepdims=True)).astype(jnp.bfloat16)


def square_sum(values):
    return jnp.einsum("...t,...t->...", values, values, preferred_element_type=jnp.float32)


def slot_cross(tmpl_block, extended, slots):
    whole = jnp.einsum("it,sejt->siej", tmpl_block, extended, preferred_element_type=jnp.float32)
    return jnp.take(whole, slots, axis=2)


def project(plan, extended, slots):
    places = (slots[:, None] == jnp.arange(extended.shape[1], dtype=jnp.int32)[None, :]).astype(
        jnp.float32
    )
    folded = jnp.einsum(
        "sikj,ke->siej", plan.astype(jnp.float32), places, precision=lax.Precision.HIGHEST
    )
    upper = folded.astype(jnp.bfloat16)
    lower = (folded - upper.astype(jnp.float32)).astype(jnp.bfloat16)
    total = jnp.einsum("siej,sejt->it", upper, extended, preferred_element_type=jnp.float32)
    return total + jnp.einsum("siej,sejt->it", lower, extended, preferred_element_type=jnp.float32)


def subject_mean(moved, count):
    total = over_copies(moved, "subj")
    return (total / count).astype(jnp.bfloat16)


def on_device(subject_data, template, neighbours, valid):
    blocks_here = template.shape[0]
    share = blocks_here // lax.axis_size("tm")
    subjects_all = subject_data.shape[0] * lax.axis_size("subj")
    offsets = neighbours - (lax.axis_index("slab") - 1) * blocks_here
    mask_all = valid.astype(jnp.float32)
    first = lax.axis_index("tm") * share
    my_offsets = lax.dynamic_slice_in_dim(offsets, first, share, 0)
    my_mask = lax.dynamic_slice_in_dim(mask_all, first, share, 0)
    full_time = gather_directly(subject_data, "tm", 3)
    extended = with_halo(full_time, (("slab", 1),), blocks_here)
    mine = lax.all_to_all(template, "tm", split_axis=0, concat_axis=2, tiled=True)
    col_norm = lax.rsqrt(square_sum(extended) + 1e-06)
    row_norm = lax.rsqrt(square_sum(mine) + 1e-06)

    def one_block(inputs):
        tmpl_block, scale_rows, slots, mask = inputs
        cross = slot_cross(tmpl_block, extended, slots)
        plan = balance(cross, scale_rows, jnp.take(col_norm, slots, axis=1), mask)
        return project(plan, extended, slots)

    moved = lax.map(one_block, (mine, row_norm, my_offsets, my_mask))
    averaged = subject_mean(moved, subjects_all)
    return exchange_in_pieces(averaged, "tm", 2, 2, 0)


def solution(mesh):
    placed = (
        P("subj", "slab", None, "tm"),
        P("slab", None, "tm"),
        P("slab", None),
        P("slab", None),
    )
    return jax.shard_map(
        on_device, mesh=mesh, in_specs=placed, out_specs=P("slab", None, "tm"), check_vma=False
    )
```

profile of v0, /device:TPU:2, one launch (start us, length us, event | category | flops | bytes accessed | tf_op | source)
XLA Modules:
  0.0 117.3 jit_solution(14926200425164752471)
XLA Ops:
  0.0 2.2 %broadcast_in_dim.73 = bf16[2,1,2,128,1024]{4,3,2,1,0:T(8,128)(2,1)} broadcast(bf16[2,128,1024]{2,1,0:T(8,128)(2,1)} %bitcast.117), dimensions={2,3,4} | broadcast | bytes 1572864 | tf_op jit(solution)/shard_map/broadcast_in_dim | solution.py:11
  2.2 3.6 %all-to-all-start = ((bf16[2,1,2,128,1024]{4,3,2,1,0:T(8,128)(2,1)}), bf16[2,1,2,128,1024]{4,3,2,1,0:T(8,128)(2,1)S(1)}, u32[]{:S(2)}, u32[]{:S(2)}) async-start(bf16[2,1,2,128,1024]{4,3,2,1,0:T(8,128)(2,1)} %broadcast_in_dim.73), calls=%async_computation | async-start | bytes 2097152 | tf_op jit(solution)/shard_map/all_to_all | solution.py:11
  5.7 0.0 copy-start
  5.8 0.0 copy-start.1
  5.8 15.3 %all-to-all-done = bf16[2,1,2,128,1024]{4,3,2,1,0:T(8,128)(2,1)S(1)} async-done(((bf16[2,1,2,128,1024]{4,3,2,1,0:T(8,128)(2,1)}), bf16[2,1,2,128,1024]{4,3,2,1,0:T(8,128)(2,1)S(1)}, u32[]{:S(2)}, u32[]{:S(2)}) %all-to-all-start) | async-done | bytes 1048608 | tf_op jit(solution)/shard_map/all_to_all | solution.py:11
  21.1 3.5 %all-to-all-start.1 = ((bf16[2,128,1024]{2,1,0:T(8,128)(2,1)}), bf16[2,128,1024]{2,1,0:T(8,128)(2,1)S(1)}, u32[]{:S(2)}, u32[]{:S(2)}) async-start(bf16[2,128,1024]{2,1,0:T(8,128)(2,1)} %param.5), calls=%async_computation.1 | async-start | bytes 1048576 | tf_op jit(solution)/shard_map/all_to_all | solution.py:119
  24.6 0.1 copy.37
  24.7 10.6 %collective-permute-start.1 = (bf16[1,2,128,2048]{3,2,1,0:T(8,128)(2,1)S(1)}, bf16[1,2,128,2048]{3,2,1,0:T(8,128)(2,1)}, u32[]{:S(2)}, u32[]{:S(2)}) collective-permute-start(bf16[1,2,128,2048]{3,2,1,0:T(8,128)(2,1)S(1)} %bitcast.108), channel_id=1, source_target_pairs={{4,0},{8,4},{12,8},{16,12},{20,16},{24,20},{28,24},{32,28},{36,32}... | collective-permute-start | bytes 3145736 | tf_op jit(solution)/shard_map/ppermute | solution.py:39
  35.3 1.9 %collective-permute-start = (bf16[1,2,128,2048]{3,2,1,0:T(8,128)(2,1)S(1)}, bf16[1,2,128,2048]{3,2,1,0:T(8,128)(2,1)}, u32[]{:S(2)}, u32[]{:S(2)}) collective-permute-start(bf16[1,2,128,2048]{3,2,1,0:T(8,128)(2,1)S(1)} %bitcast.109), channel_id=1, source_target_pairs={{0,4},{4,8},{8,12},{12,16},{16,20},{20,24},{24,28},{28,32},{32,36}... | collective-permute-start | bytes 3145736 | tf_op jit(solution)/shard_map/ppermute | solution.py:37
  37.3 0.6 fusion.24
  38.7 0.5 copy.22
  39.2 0.4 reshape.364
  39.6 0.1 copy.38
  39.7 0.2 fusion.15
  39.9 16.6 %collective-permute-done.1 = bf16[1,2,128,2048]{3,2,1,0:T(8,128)(2,1)} collective-permute-done((bf16[1,2,128,2048]{3,2,1,0:T(8,128)(2,1)S(1)}, bf16[1,2,128,2048]{3,2,1,0:T(8,128)(2,1)}, u32[]{:S(2)}, u32[]{:S(2)}) %collective-permute-start.1) | collective-permute-done | bytes 1048608 | tf_op jit(solution)/shard_map/ppermute | solution.py:39
  56.5 8.4 %collective-permute-done = bf16[1,2,128,2048]{3,2,1,0:T(8,128)(2,1)} collective-permute-done((bf16[1,2,128,2048]{3,2,1,0:T(8,128)(2,1)S(1)}, bf16[1,2,128,2048]{3,2,1,0:T(8,128)(2,1)}, u32[]{:S(2)}, u32[]{:S(2)}) %collective-permute-start) | collective-permute-done | bytes 1048608 | tf_op jit(solution)/shard_map/ppermute | solution.py:37
  65.0 2.0 %fusion = f32[6,128]{1,0:T(8,128)S(1)} fusion(bf16[1,2,128,2048]{3,2,1,0:T(8,128)(2,1)} %collective-permute-done.1, bf16[1,2,128,2048]{3,2,1,0:T(8,128)(2,1)S(1)} %bitcast.110, bf16[1,2,128,2048]{3,2,1,0:T(8,128)(2,1)} %collective-permute-done), kind=kLoop, calls=%fused_computation.3 | loop fusion | flops 7863552 | bytes 3148800 | tf_op jit(solution)/shard_map/...t,...t->.../dot_general | solution.py:82
  67.0 0.6 gather_fusion.1
  67.5 2.5 %convolution_bitcast_fusion.3 = f32[128,6,128]{0,2,1:T(8,128)S(1)} fusion(bf16[128,2048,1]{1,0,2:T(8,128)(2,1)S(1)} %reshape.364, bf16[1,2,128,2048]{3,2,1,0:T(8,128)(2,1)} %collective-permute-done.1, bf16[1,2,128,2048]{3,2,1,0:T(8,128)(2,1)S(1)} %bitcast.111, bf16[1,2,128,2048]{3,2,1,0:T(8,128)(2,1)} %collective-permute-done), kind=kOutput, calls=%fused_computation.30 | convolution fusion | flops 405798912 | bytes 4063232 | tf_op jit(solution)/shard_map/while/body/eval_jaxpr/it,sejt->siej/dot_general | solution.py:86
  70.1 0.7 gather_fusion
  70.7 0.1 broadcast_select_fusion
  70.8 0.8 fusion.26
  71.6 1.4 %multiply_reduce_fusion.5 = f32[27,128]{1,0:T(8,128)S(1)} fusion(f32[128]{0:T(128)S(1)} %broadcast_divide_fusion.2, f32[27]{0:T(128)S(1)} %get-tuple-element.20, f32[27,128]{1,0:T(8,128)S(1)} %broadcast_select_fusion, f32[128]{0:T(128)S(1)} %add_rsqrt_fusion.1, f32[27,128,128]{1,2,0:T(8,128)S(1)} %gather_fusion, pred[27]{0:T(512)(128)(4,1)S(1)} %get-tuple-element.21), kind=kLoop, calls=%fused_computation.27 | loop fusion | flops 3093120 | bytes 1798279 | tf_op jit(solution)/shard_map/while/body/eval_jaxpr/reduce_sum | solution.py:76
  73.0 0.1 add_divide_fusion.2
  73.1 1.3 %multiply_reduce_fusion.4 = f32[128]{0:T(128)S(1)} fusion(f32[27,128]{1,0:T(8,128)S(1)} %add_divide_fusion.2, f32[27]{0:T(128)S(1)} %get-tuple-element.20, f32[27,128]{1,0:T(8,128)S(1)} %broadcast_select_fusion, f32[128]{0:T(128)S(1)} %add_rsqrt_fusion.1, f32[27,128,128]{1,2,0:T(8,128)S(1)} %gather_fusion, pred[27]{0:T(512)(128)(4,1)S(1)} %get-tuple-element.21), kind=kLoop, calls=%fused_computation.26 | loop fusion | flops 3096448 | bytes 1798279 | tf_op jit(solution)/shard_map/while/body/eval_jaxpr/reduce_sum | solution.py:75
  74.4 1.4 %multiply_reduce_fusion.3 = f32[27,128]{1,0:T(8,128)S(1)} fusion(f32[128]{0:T(128)S(1)} %broadcast_divide_fusion.1, f32[27]{0:T(128)S(1)} %get-tuple-element.20, f32[27,128]{1,0:T(8,128)S(1)} %broadcast_select_fusion, f32[128]{0:T(128)S(1)} %add_rsqrt_fusion.1, f32[27,128,128]{1,2,0:T(8,128)S(1)} %gather_fusion, pred[27]{0:T(512)(128)(4,1)S(1)} %get-tuple-element.21), kind=kLoop, calls=%fused_computation.25 | loop fusion | flops 3093120 | bytes 1798279 | tf_op jit(solution)/shard_map/while/body/eval_jaxpr/reduce_sum | solution.py:76
  75.8 0.1 add_divide_fusion.1
  75.9 1.3 %multiply_reduce_fusion.2 = f32[128]{0:T(128)S(1)} fusion(f32[27,128]{1,0:T(8,128)S(1)} %add_divide_fusion.1, f32[27]{0:T(128)S(1)} %get-tuple-element.20, f32[27,128]{1,0:T(8,128)S(1)} %broadcast_select_fusion, f32[128]{0:T(128)S(1)} %add_rsqrt_fusion.1, f32[27,128,128]{1,2,0:T(8,128)S(1)} %gather_fusion, pred[27]{0:T(512)(128)(4,1)S(1)} %get-tuple-element.21), kind=kLoop, calls=%fused_computation.24 | loop fusion | flops 3096448 | bytes 1798279 | tf_op jit(solution)/shard_map/while/body/eval_jaxpr/reduce_sum | solution.py:75
  77.3 1.4 %multiply_reduce_fusion.1 = f32[27,128]{1,0:T(8,128)S(1)} fusion(f32[128]{0:T(128)S(1)} %broadcast_divide_fusion, f32[27]{0:T(128)S(1)} %get-tuple-element.20, f32[27,128]{1,0:T(8,128)S(1)} %broadcast_select_fusion, f32[128]{0:T(128)S(1)} %add_rsqrt_fusion.1, f32[27,128,128]{1,2,0:T(8,128)S(1)} %gather_fusion, pred[27]{0:T(512)(128)(4,1)S(1)} %get-tuple-element.21), kind=kLoop, calls=%fused_computation.23 | loop fusion | flops 3093120 | bytes 1798279 | tf_op jit(solution)/shard_map/while/body/eval_jaxpr/reduce_sum | solution.py:76
  78.6 0.1 add_divide_fusion
  78.7 1.3 %multiply_reduce_fusion = f32[128]{0:T(128)S(1)} fusion(f32[27,128]{1,0:T(8,128)S(1)} %add_divide_fusion, f32[27]{0:T(128)S(1)} %get-tuple-element.20, f32[27,128]{1,0:T(8,128)S(1)} %broadcast_select_fusion, f32[128]{0:T(128)S(1)} %add_rsqrt_fusion.1, f32[27,128,128]{1,2,0:T(8,128)S(1)} %gather_fusion, pred[27]{0:T(512)(128)(4,1)S(1)} %get-tuple-element.21), kind=kLoop, calls=%fused_computation.22 | loop fusion | flops 3096448 | bytes 1798279 | tf_op jit(solution)/shard_map/while/body/eval_jaxpr/reduce_sum | solution.py:78
  80.1 2.3 %fusion.14 = bf16[128,27,128]{0,2,1:T(8,128)(2,1)} fusion(f32[27,128,128]{1,2,0:T(8,128)S(1)} %gather_fusion, f32[128]{0:T(128)S(1)} %multiply_reduce_fusion, f32[27,128]{1,0:T(8,128)S(1)} %add_divide_fusion, f32[27]{0:T(128)S(1)} %get-tuple-element.20, f32[27,128]{1,0:T(8,128)S(1)} %broadcast_select_fusion, f32[128]{0:T(128)S(1)} %add_rsqrt_fusion.1, ...), kind=kLoop, calls=%fused_computation.28 | loop fusion | flops 3538944 | bytes 2683015 | tf_op jit(solution)/shard_map/while/body/eval_jaxpr/convert_element_type | solution.py:78
  82.4 1.9 %copy.23 = bf16[128,27,128]{2,1,0:T(8,128)(2,1)S(1)} copy(bf16[128,27,128]{0,2,1:T(8,128)(2,1)} %fusion.14) | data formatting | bytes 1769472 | tf_op jit(solution)/shard_map/while/body/eval_jaxpr/convert_element_type | solution.py:78
  84.3 0.3 convert_bitcast_fusion
  84.6 2.3 %convolution_bitcast_fusion = f32[128,2048]{1,0:T(8,128)S(1)} fusion(bf16[128,6,128]{2,1,0:T(8,128)(2,1)S(1)} %get-tuple-element.36, bf16[1,2,128,2048]{3,2,1,0:T(8,128)(2,1)} %collective-permute-done.1, bf16[1,2,128,2048]{3,2,1,0:T(8,128)(2,1)S(1)} %bitcast.112, bf16[1,2,128,2048]{3,2,1,0:T(8,128)(2,1)} %collective-permute-done), kind=kOutput, calls=%fused_computation.5 | convolution fusion | flops 405798912 | bytes 4390912 | tf_op jit(solution)/shard_map/while/body/eval_jaxpr/siej,sejt->it/dot_general | solution.py:100
  86.9 2.3 %fusion.1 = f32[128,2048]{1,0:T(8,128)S(1)} fusion(f32[128,2048]{1,0:T(8,128)S(1)} %convolution_bitcast_fusion, bf16[128,6,128]{2,1,0:T(8,128)(2,1)S(1)} %get-tuple-element.34, bf16[1,2,128,2048]{3,2,1,0:T(8,128)(2,1)} %collective-permute-done.1, bf16[1,2,128,2048]{3,2,1,0:T(8,128)(2,1)S(1)} %bitcast.113, bf16[1,2,128,2048]{3,2,1,0:T(8,128)(2,1)} %collective-permute-done), kind=kOutput, calls=%fused_computation.7 | convolution fusion | flops 406061056 | bytes 5439488 | tf_op jit(solution)/shard_map/while/body/eval_jaxpr/siej,sejt->it/dot_general | solution.py:99
  89.2 0.2 broadcast_in_dim.79
  89.4 5.4 %all_to_all.35 = f32[2,1,128,2048]{3,2,1,0:T(8,128)S(1)} all-to-all(f32[2,1,128,2048]{3,2,1,0:T(8,128)S(1)} %broadcast_in_dim.79), channel_id=1, replica_groups=mesh['slab'=64,'subj'=2,'tm'=2] {'subj'}, dimensions={0} | all-to-all | bytes 4194304 | tf_op jit(solution)/shard_map/all_to_all | solution.py:11
  94.8 0.2 reduce_sum.97
  95.1 0.1 multiply_convert_fusion
  95.1 0.3 copy.26
  95.4 0.2 fusion.29
  95.6 0.9 copy.27
  96.5 3.9 %all-to-all-start.3 = ((bf16[2,1,64,1024]{3,2,1,0:T(8,128)(2,1)}), bf16[2,1,64,1024]{3,2,1,0:T(8,128)(2,1)S(1)}, u32[]{:S(2)}, u32[]{:S(2)}) async-start(bf16[2,1,64,1024]{3,2,1,0:T(8,128)(2,1)} %copy.27), calls=%async_computation.3 | async-start | bytes 524288 | tf_op jit(solution)/shard_map/all_to_all | solution.py:62
  100.4 0.2 copy.28
  100.6 6.8 %all-to-all-done.3 = bf16[2,1,64,1024]{3,2,1,0:T(8,128)(2,1)S(1)} async-done(((bf16[2,1,64,1024]{3,2,1,0:T(8,128)(2,1)}), bf16[2,1,64,1024]{3,2,1,0:T(8,128)(2,1)S(1)}, u32[]{:S(2)}, u32[]{:S(2)}) %all-to-all-start.3) | async-done | bytes 262176 | tf_op jit(solution)/shard_map/all_to_all | solution.py:62
  107.4 9.1 %all_to_all.36 = bf16[2,1,64,1024]{3,2,1,0:T(8,128)(2,1)S(1)} all-to-all(bf16[2,1,64,1024]{3,2,1,0:T(8,128)(2,1)S(1)} %copy.28), channel_id=1, replica_groups=mesh['slab'=64,'subj'=2,'tm'=2] {'tm'}, dimensions={0} | all-to-all | bytes 524288 | tf_op jit(solution)/shard_map/all_to_all | solution.py:62
  116.4 0.8 maximum_bitcast_fusion.1
  (15 shorter events, 0.1 us)
Async XLA Ops:
  2.2 18.9 %all-to-all-start = ((bf16[2,1,2,128,1024]{4,3,2,1,0:T(8,128)(2,1)}), bf16[2,1,2,128,1024]{4,3,2,1,0:T(8,128)(2,1)S(1)}, u32[]{:S(2)}, u32[]{:S(2)}) async-start(bf16[2,1,2,128,1024]{4,3,2,1,0:T(8,128)(2,1)} %broadcast_in_dim.73), calls=%async_computation | async-start | bytes 2097152 | tf_op jit(solution)/shard_map/all_to_all | solution.py:11
  5.7 31.5 %copy-start = (s32[2,27]{1,0:T(2,128)S(1)}, s32[2,27]{1,0:T(2,128)}, u32[]{:S(2)}) copy-start(s32[2,27]{1,0:T(2,128)} %param.6) | copy-start | bytes 652
  5.8 31.5 %copy-start.1 = (s32[2,27]{1,0:T(2,128)S(1)}, s32[2,27]{1,0:T(2,128)}, u32[]{:S(2)}) copy-start(s32[2,27]{1,0:T(2,128)} %param.7) | copy-start | bytes 652
  21.1 17.6 %all-to-all-start.1 = ((bf16[2,128,1024]{2,1,0:T(8,128)(2,1)}), bf16[2,128,1024]{2,1,0:T(8,128)(2,1)S(1)}, u32[]{:S(2)}, u32[]{:S(2)}) async-start(bf16[2,128,1024]{2,1,0:T(8,128)(2,1)} %param.5), calls=%async_computation.1 | async-start | bytes 1048576 | tf_op jit(solution)/shard_map/all_to_all | solution.py:119
  24.7 31.8 %collective-permute-start.1 = (bf16[1,2,128,2048]{3,2,1,0:T(8,128)(2,1)S(1)}, bf16[1,2,128,2048]{3,2,1,0:T(8,128)(2,1)}, u32[]{:S(2)}, u32[]{:S(2)}) collective-permute-start(bf16[1,2,128,2048]{3,2,1,0:T(8,128)(2,1)S(1)} %bitcast.108), channel_id=1, source_target_pairs={{4,0},{8,4},{12,8},{16,12},{20,16},{24,20},{28,24},{32,28},{36,32}... | collective-permute-start | bytes 3145736 | tf_op jit(solution)/shard_map/ppermute | solution.py:39
  35.3 29.6 %collective-permute-start = (bf16[1,2,128,2048]{3,2,1,0:T(8,128)(2,1)S(1)}, bf16[1,2,128,2048]{3,2,1,0:T(8,128)(2,1)}, u32[]{:S(2)}, u32[]{:S(2)}) collective-permute-start(bf16[1,2,128,2048]{3,2,1,0:T(8,128)(2,1)S(1)} %bitcast.109), channel_id=1, source_target_pairs={{0,4},{4,8},{8,12},{12,16},{16,20},{20,24},{24,28},{28,32},{32,36}... | collective-permute-start | bytes 3145736 | tf_op jit(solution)/shard_map/ppermute | solution.py:37
  96.5 10.9 %all-to-all-start.3 = ((bf16[2,1,64,1024]{3,2,1,0:T(8,128)(2,1)}), bf16[2,1,64,1024]{3,2,1,0:T(8,128)(2,1)S(1)}, u32[]{:S(2)}, u32[]{:S(2)}) async-start(bf16[2,1,64,1024]{3,2,1,0:T(8,128)(2,1)} %copy.27), calls=%async_computation.3 | async-start | bytes 524288 | tf_op jit(solution)/shard_map/all_to_all | solution.py:62
where the time goes:
time: 118 us; the launch traced here: 117 us
  waiting for transfers between devices  47.2 us (40%)
  starting transfers between devices  23.5 us (20%)
  other arithmetic  15.5 us (13%)
  blocking collectives  14.5 us (12%)
  local copies, waits for them, and re-layouts  8.28 us (7%)
  matrix products  7.33 us (6%)
    ppermute x1, waiting for transfers between devices, with_halo(): lax.ppermute(head, axis, [((i + 1) % count, i) for i in range(ends)])  16.6 us
    all_to_all x1, waiting for transfers between devices, from_everyone(): lax.all_to_all(jnp.broadcast_to(x[None], (size, *x.shape)), axis, 0, 0, t...  15.3 us
    ppermute x1, starting transfers between devices, with_halo(): lax.ppermute(head, axis, [((i + 1) % count, i) for i in range(ends)])  10.6 us
    all_to_all x1, blocking collectives, exchange_in_pieces(): lax.all_to_all(piece, axis, split_axis=0, concat_axis=0, tiled=True)  9.06 us
    ppermute x1, waiting for transfers between devices, with_halo(): lax.ppermute(tail, axis, [(i, (i + 1) % count) for i in range(ends)])  8.44 us
    all_to_all x1, waiting for transfers between devices, exchange_in_pieces(): lax.all_to_all(piece, axis, split_axis=0, concat_axis=0, tiled=True)  6.77 us
    all_to_all x1, blocking collectives, from_everyone(): lax.all_to_all(jnp.broadcast_to(x[None], (size, *x.shape)), axis, 0, 0, t...  5.42 us
    reduce_sum x3, other arithmetic, balance(): jnp.sum(kernel * row_weight, axis=1, keepdims=True) + filler  4.12 us
  transfers between devices with their start and end apart: 5, of which 4 were waited for; matrix products, arithmetic and copies ran while one was open for 2% of the time, Pallas kernels for 0%

commit v1 on v0

--- a/solution.py
+++ b/solution.py
@@ -116,7 +116,10 @@
     my_mask = lax.dynamic_slice_in_dim(mask_all, first, share, 0)
     full_time = gather_directly(subject_data, "tm", 3)
     extended = with_halo(full_time, (("slab", 1),), blocks_here)
-    mine = lax.all_to_all(template, "tm", split_axis=0, concat_axis=2, tiled=True)
+    mine = jnp.concatenate(
+        lax.all_to_all(jnp.stack(jnp.split(template, lax.axis_size("tm"), axis=0)), "tm", 0, 0),
+        axis=2,
+    )
     col_norm = lax.rsqrt(square_sum(extended) + 1e-06)
     row_norm = lax.rsqrt(square_sum(mine) + 1e-06)
 

time: 118 us -> 118 us (level)
  transfers between devices with their start and end apart: 5 -> 5, of which waited for: 4 -> 4; matrix products, arithmetic and copies ran while one was open for 2% -> 3% of each run, Pallas kernels for 0% -> 0%
where the time goes in v1:
time: 118 us; the launch traced here: 117 us
  waiting for transfers between devices  46.3 us (39%)
  starting transfers between devices  23.5 us (20%)
  other arithmetic  16.4 us (14%)
  blocking collectives  14.5 us (12%)
  local copies, waits for them, and re-layouts  8.37 us (7%)
  matrix products  7.33 us (6%)
    ppermute x1, waiting for transfers between devices, with_halo(): lax.ppermute(head, axis, [((i + 1) % count, i) for i in range(ends)])  16.6 us
    all_to_all x1, waiting for transfers between devices, from_everyone(): lax.all_to_all(jnp.broadcast_to(x[None], (size, *x.shape)), axis, 0, 0, t...  14.5 us
    ppermute x1, starting transfers between devices, with_halo(): lax.ppermute(head, axis, [((i + 1) % count, i) for i in range(ends)])  10.6 us
    all_to_all x1, blocking collectives, exchange_in_pieces(): lax.all_to_all(piece, axis, split_axis=0, concat_axis=0, tiled=True)  9.06 us
    ppermute x1, waiting for transfers between devices, with_halo(): lax.ppermute(tail, axis, [(i, (i + 1) % count) for i in range(ends)])  8.44 us
    all_to_all x1, waiting for transfers between devices, exchange_in_pieces(): lax.all_to_all(piece, axis, split_axis=0, concat_axis=0, tiled=True)  6.77 us
    all_to_all x1, blocking collectives, from_everyone(): lax.all_to_all(jnp.broadcast_to(x[None], (size, *x.shape)), axis, 0, 0, t...  5.42 us
    reduce_sum x3, other arithmetic, balance(): jnp.sum(kernel * row_weight, axis=1, keepdims=True) + filler  4.12 us
  transfers between devices with their start and end apart: 5, of which 4 were waited for; matrix products, arithmetic and copies ran while one was open for 3% of the time, Pallas kernels for 0%

profile of v1, /device:TPU:2, one launch (start us, length us, event | category | flops | bytes accessed | tf_op | source)
XLA Modules:
  0.0 117.3 jit_solution(8858030117045173728)
XLA Ops:
  0.0 2.2 %broadcast_in_dim.73 = bf16[2,1,2,128,1024]{4,3,2,1,0:T(8,128)(2,1)} broadcast(bf16[2,128,1024]{2,1,0:T(8,128)(2,1)} %bitcast.119), dimensions={2,3,4} | broadcast | bytes 1572864 | tf_op jit(solution)/shard_map/broadcast_in_dim | solution.py:11
  2.2 3.6 %all-to-all-start = ((bf16[2,1,2,128,1024]{4,3,2,1,0:T(8,128)(2,1)}), bf16[2,1,2,128,1024]{4,3,2,1,0:T(8,128)(2,1)S(1)}, u32[]{:S(2)}, u32[]{:S(2)}) async-start(bf16[2,1,2,128,1024]{4,3,2,1,0:T(8,128)(2,1)} %broadcast_in_dim.73), calls=%async_computation | async-start | bytes 2097152 | tf_op jit(solution)/shard_map/all_to_all | solution.py:11
  5.9 0.8 pad_maximum_fusion
  6.7 14.5 %all-to-all-done = bf16[2,1,2,128,1024]{4,3,2,1,0:T(8,128)(2,1)S(1)} async-done(((bf16[2,1,2,128,1024]{4,3,2,1,0:T(8,128)(2,1)}), bf16[2,1,2,128,1024]{4,3,2,1,0:T(8,128)(2,1)S(1)}, u32[]{:S(2)}, u32[]{:S(2)}) %all-to-all-start) | async-done | bytes 1048608 | tf_op jit(solution)/shard_map/all_to_all | solution.py:11
  21.2 3.5 %all-to-all-start.1 = ((bf16[2,1,128,1024]{3,2,1,0:T(8,128)(2,1)}), bf16[2,1,128,1024]{3,2,1,0:T(8,128)(2,1)S(1)}, u32[]{:S(2)}, u32[]{:S(2)}) async-start(bf16[2,1,128,1024]{3,2,1,0:T(8,128)(2,1)} %pad_maximum_fusion), calls=%async_computation.1 | async-start | bytes 1048576 | tf_op jit(solution)/shard_map/all_to_all | solution.py:120
  24.7 0.1 copy.37
  24.8 10.6 %collective-permute-start.1 = (bf16[1,2,128,2048]{3,2,1,0:T(8,128)(2,1)S(1)}, bf16[1,2,128,2048]{3,2,1,0:T(8,128)(2,1)}, u32[]{:S(2)}, u32[]{:S(2)}) collective-permute-start(bf16[1,2,128,2048]{3,2,1,0:T(8,128)(2,1)S(1)} %bitcast.110), channel_id=1, source_target_pairs={{4,0},{8,4},{12,8},{16,12},{20,16},{24,20},{28,24},{32,28},{36,32}... | collective-permute-start | bytes 3145736 | tf_op jit(solution)/shard_map/ppermute | solution.py:39
  35.4 1.9 %collective-permute-start = (bf16[1,2,128,2048]{3,2,1,0:T(8,128)(2,1)S(1)}, bf16[1,2,128,2048]{3,2,1,0:T(8,128)(2,1)}, u32[]{:S(2)}, u32[]{:S(2)}) collective-permute-start(bf16[1,2,128,2048]{3,2,1,0:T(8,128)(2,1)S(1)} %bitcast.111), channel_id=1, source_target_pairs={{0,4},{4,8},{8,12},{12,16},{16,20},{20,24},{24,28},{28,32},{32,36}... | collective-permute-start | bytes 3145736 | tf_op jit(solution)/shard_map/ppermute | solution.py:37
  37.4 0.6 fusion.24
  38.7 0.0 all-to-all-done.1
  38.7 0.5 copy.22
  39.3 0.4 reshape.369
  39.6 0.1 copy.38
  39.8 0.2 fusion.15
  40.0 16.6 %collective-permute-done.1 = bf16[1,2,128,2048]{3,2,1,0:T(8,128)(2,1)} collective-permute-done((bf16[1,2,128,2048]{3,2,1,0:T(8,128)(2,1)S(1)}, bf16[1,2,128,2048]{3,2,1,0:T(8,128)(2,1)}, u32[]{:S(2)}, u32[]{:S(2)}) %collective-permute-start.1) | collective-permute-done | bytes 1048608 | tf_op jit(solution)/shard_map/ppermute | solution.py:39
  56.6 8.4 %collective-permute-done = bf16[1,2,128,2048]{3,2,1,0:T(8,128)(2,1)} collective-permute-done((bf16[1,2,128,2048]{3,2,1,0:T(8,128)(2,1)S(1)}, bf16[1,2,128,2048]{3,2,1,0:T(8,128)(2,1)}, u32[]{:S(2)}, u32[]{:S(2)}) %collective-permute-start) | collective-permute-done | bytes 1048608 | tf_op jit(solution)/shard_map/ppermute | solution.py:37
  65.0 2.0 %fusion = f32[6,128]{1,0:T(8,128)S(1)} fusion(bf16[1,2,128,2048]{3,2,1,0:T(8,128)(2,1)} %collective-permute-done.1, bf16[1,2,128,2048]{3,2,1,0:T(8,128)(2,1)S(1)} %bitcast.112, bf16[1,2,128,2048]{3,2,1,0:T(8,128)(2,1)} %collective-permute-done), kind=kLoop, calls=%fused_computation.3 | loop fusion | flops 7863552 | bytes 3148800 | tf_op jit(solution)/shard_map/...t,...t->.../dot_general | solution.py:82
  67.0 0.6 gather_fusion.1
  67.6 2.5 %convolution_bitcast_fusion.3 = f32[128,6,128]{0,2,1:T(8,128)S(1)} fusion(bf16[128,2048,1]{1,0,2:T(8,128)(2,1)S(1)} %reshape.369, bf16[1,2,128,2048]{3,2,1,0:T(8,128)(2,1)} %collective-permute-done.1, bf16[1,2,128,2048]{3,2,1,0:T(8,128)(2,1)S(1)} %bitcast.113, bf16[1,2,128,2048]{3,2,1,0:T(8,128)(2,1)} %collective-permute-done), kind=kOutput, calls=%fused_computation.30 | convolution fusion | flops 405798912 | bytes 4063232 | tf_op jit(solution)/shard_map/while/body/eval_jaxpr/it,sejt->siej/dot_general | solution.py:86
  70.1 0.7 gather_fusion
  70.8 0.1 broadcast_select_fusion
  70.9 0.8 fusion.26
  71.7 1.4 %multiply_reduce_fusion.5 = f32[27,128]{1,0:T(8,128)S(1)} fusion(f32[128]{0:T(128)S(1)} %broadcast_divide_fusion.2, f32[27]{0:T(128)S(1)} %get-tuple-element.20, f32[27,128]{1,0:T(8,128)S(1)} %broadcast_select_fusion, f32[128]{0:T(128)S(1)} %add_rsqrt_fusion.1, f32[27,128,128]{1,2,0:T(8,128)S(1)} %gather_fusion, pred[27]{0:T(512)(128)(4,1)S(1)} %get-tuple-element.21), kind=kLoop, calls=%fused_computation.27 | loop fusion | flops 3093120 | bytes 1798279 | tf_op jit(solution)/shard_map/while/body/eval_jaxpr/reduce_sum | solution.py:76
  73.1 0.1 add_divide_fusion.2
  73.1 1.3 %multiply_reduce_fusion.4 = f32[128]{0:T(128)S(1)} fusion(f32[27,128]{1,0:T(8,128)S(1)} %add_divide_fusion.2, f32[27]{0:T(128)S(1)} %get-tuple-element.20, f32[27,128]{1,0:T(8,128)S(1)} %broadcast_select_fusion, f32[128]{0:T(128)S(1)} %add_rsqrt_fusion.1, f32[27,128,128]{1,2,0:T(8,128)S(1)} %gather_fusion, pred[27]{0:T(512)(128)(4,1)S(1)} %get-tuple-element.21), kind=kLoop, calls=%fused_computation.26 | loop fusion | flops 3096448 | bytes 1798279 | tf_op jit(solution)/shard_map/while/body/eval_jaxpr/reduce_sum | solution.py:75
  74.5 1.4 %multiply_reduce_fusion.3 = f32[27,128]{1,0:T(8,128)S(1)} fusion(f32[128]{0:T(128)S(1)} %broadcast_divide_fusion.1, f32[27]{0:T(128)S(1)} %get-tuple-element.20, f32[27,128]{1,0:T(8,128)S(1)} %broadcast_select_fusion, f32[128]{0:T(128)S(1)} %add_rsqrt_fusion.1, f32[27,128,128]{1,2,0:T(8,128)S(1)} %gather_fusion, pred[27]{0:T(512)(128)(4,1)S(1)} %get-tuple-element.21), kind=kLoop, calls=%fused_computation.25 | loop fusion | flops 3093120 | bytes 1798279 | tf_op jit(solution)/shard_map/while/body/eval_jaxpr/reduce_sum | solution.py:76
  75.9 0.1 add_divide_fusion.1
  76.0 1.3 %multiply_reduce_fusion.2 = f32[128]{0:T(128)S(1)} fusion(f32[27,128]{1,0:T(8,128)S(1)} %add_divide_fusion.1, f32[27]{0:T(128)S(1)} %get-tuple-element.20, f32[27,128]{1,0:T(8,128)S(1)} %broadcast_select_fusion, f32[128]{0:T(128)S(1)} %add_rsqrt_fusion.1, f32[27,128,128]{1,2,0:T(8,128)S(1)} %gather_fusion, pred[27]{0:T(512)(128)(4,1)S(1)} %get-tuple-element.21), kind=kLoop, calls=%fused_computation.24 | loop fusion | flops 3096448 | bytes 1798279 | tf_op jit(solution)/shard_map/while/body/eval_jaxpr/reduce_sum | solution.py:75
  77.3 1.4 %multiply_reduce_fusion.1 = f32[27,128]{1,0:T(8,128)S(1)} fusion(f32[128]{0:T(128)S(1)} %broadcast_divide_fusion, f32[27]{0:T(128)S(1)} %get-tuple-element.20, f32[27,128]{1,0:T(8,128)S(1)} %broadcast_select_fusion, f32[128]{0:T(128)S(1)} %add_rsqrt_fusion.1, f32[27,128,128]{1,2,0:T(8,128)S(1)} %gather_fusion, pred[27]{0:T(512)(128)(4,1)S(1)} %get-tuple-element.21), kind=kLoop, calls=%fused_computation.23 | loop fusion | flops 3093120 | bytes 1798279 | tf_op jit(solution)/shard_map/while/body/eval_jaxpr/reduce_sum | solution.py:76
  78.7 0.1 add_divide_fusion
  78.8 1.3 %multiply_reduce_fusion = f32[128]{0:T(128)S(1)} fusion(f32[27,128]{1,0:T(8,128)S(1)} %add_divide_fusion, f32[27]{0:T(128)S(1)} %get-tuple-element.20, f32[27,128]{1,0:T(8,128)S(1)} %broadcast_select_fusion, f32[128]{0:T(128)S(1)} %add_rsqrt_fusion.1, f32[27,128,128]{1,2,0:T(8,128)S(1)} %gather_fusion, pred[27]{0:T(512)(128)(4,1)S(1)} %get-tuple-element.21), kind=kLoop, calls=%fused_computation.22 | loop fusion | flops 3096448 | bytes 1798279 | tf_op jit(solution)/shard_map/while/body/eval_jaxpr/reduce_sum | solution.py:78
  80.1 2.3 %fusion.14 = bf16[128,27,128]{0,2,1:T(8,128)(2,1)} fusion(f32[27,128,128]{1,2,0:T(8,128)S(1)} %gather_fusion, f32[128]{0:T(128)S(1)} %multiply_reduce_fusion, f32[27,128]{1,0:T(8,128)S(1)} %add_divide_fusion, f32[27]{0:T(128)S(1)} %get-tuple-element.20, f32[27,128]{1,0:T(8,128)S(1)} %broadcast_select_fusion, f32[128]{0:T(128)S(1)} %add_rsqrt_fusion.1, ...), kind=kLoop, calls=%fused_computation.28 | loop fusion | flops 3538944 | bytes 2683015 | tf_op jit(solution)/shard_map/while/body/eval_jaxpr/convert_element_type | solution.py:78
  82.4 1.9 %copy.23 = bf16[128,27,128]{2,1,0:T(8,128)(2,1)S(1)} copy(bf16[128,27,128]{0,2,1:T(8,128)(2,1)} %fusion.14) | data formatting | bytes 1769472 | tf_op jit(solution)/shard_map/while/body/eval_jaxpr/convert_element_type | solution.py:78
  84.4 0.3 convert_bitcast_fusion
  84.6 2.3 %convolution_bitcast_fusion = f32[128,2048]{1,0:T(8,128)S(1)} fusion(bf16[128,6,128]{2,1,0:T(8,128)(2,1)S(1)} %get-tuple-element.36, bf16[1,2,128,2048]{3,2,1,0:T(8,128)(2,1)} %collective-permute-done.1, bf16[1,2,128,2048]{3,2,1,0:T(8,128)(2,1)S(1)} %bitcast.114, bf16[1,2,128,2048]{3,2,1,0:T(8,128)(2,1)} %collective-permute-done), kind=kOutput, calls=%fused_computation.5 | convolution fusion | flops 405798912 | bytes 4390912 | tf_op jit(solution)/shard_map/while/body/eval_jaxpr/siej,sejt->it/dot_general | solution.py:100
  86.9 2.3 %fusion.1 = f32[128,2048]{1,0:T(8,128)S(1)} fusion(f32[128,2048]{1,0:T(8,128)S(1)} %convolution_bitcast_fusion, bf16[128,6,128]{2,1,0:T(8,128)(2,1)S(1)} %get-tuple-element.34, bf16[1,2,128,2048]{3,2,1,0:T(8,128)(2,1)} %collective-permute-done.1, bf16[1,2,128,2048]{3,2,1,0:T(8,128)(2,1)S(1)} %bitcast.115, bf16[1,2,128,2048]{3,2,1,0:T(8,128)(2,1)} %collective-permute-done), kind=kOutput, calls=%fused_computation.7 | convolution fusion | flops 406061056 | bytes 5439488 | tf_op jit(solution)/shard_map/while/body/eval_jaxpr/siej,sejt->it/dot_general | solution.py:99
  89.2 0.2 broadcast_in_dim.79
  89.5 5.4 %all_to_all.25 = f32[2,1,128,2048]{3,2,1,0:T(8,128)S(1)} all-to-all(f32[2,1,128,2048]{3,2,1,0:T(8,128)S(1)} %broadcast_in_dim.79), channel_id=1, replica_groups=mesh['slab'=64,'subj'=2,'tm'=2] {'subj'}, dimensions={0} | all-to-all | bytes 4194304 | tf_op jit(solution)/shard_map/all_to_all | solution.py:11
  94.9 0.2 reduce_sum.97
  95.1 0.1 multiply_convert_fusion
  95.2 0.3 copy.26
  95.5 0.2 fusion.29
  95.7 0.9 copy.27
  96.6 3.9 %all-to-all-start.3 = ((bf16[2,1,64,1024]{3,2,1,0:T(8,128)(2,1)}), bf16[2,1,64,1024]{3,2,1,0:T(8,128)(2,1)S(1)}, u32[]{:S(2)}, u32[]{:S(2)}) async-start(bf16[2,1,64,1024]{3,2,1,0:T(8,128)(2,1)} %copy.27), calls=%async_computation.3 | async-start | bytes 524288 | tf_op jit(solution)/shard_map/all_to_all | solution.py:62
  100.5 0.2 copy.28
  100.7 6.8 %all-to-all-done.3 = bf16[2,1,64,1024]{3,2,1,0:T(8,128)(2,1)S(1)} async-done(((bf16[2,1,64,1024]{3,2,1,0:T(8,128)(2,1)}), bf16[2,1,64,1024]{3,2,1,0:T(8,128)(2,1)S(1)}, u32[]{:S(2)}, u32[]{:S(2)}) %all-to-all-start.3) | async-done | bytes 262176 | tf_op jit(solution)/shard_map/all_to_all | solution.py:62
  107.4 9.1 %all_to_all.26 = bf16[2,1,64,1024]{3,2,1,0:T(8,128)(2,1)S(1)} all-to-all(bf16[2,1,64,1024]{3,2,1,0:T(8,128)(2,1)S(1)} %copy.28), channel_id=1, replica_groups=mesh['slab'=64,'subj'=2,'tm'=2] {'tm'}, dimensions={0} | all-to-all | bytes 524288 | tf_op jit(solution)/shard_map/all_to_all | solution.py:62
  116.5 0.8 maximum_bitcast_fusion.1
  (19 shorter events, 0.1 us)
Async XLA Ops:
  0.0 5.8 %copy-start = (bf16[2,128,1024]{2,1,0:T(8,128)(2,1)S(1)}, bf16[2,128,1024]{2,1,0:T(8,128)(2,1)}, u32[]{:S(2)}) copy-start(bf16[2,128,1024]{2,1,0:T(8,128)(2,1)} %param.5) | copy-start | bytes 1572868
  2.2 18.9 %all-to-all-start = ((bf16[2,1,2,128,1024]{4,3,2,1,0:T(8,128)(2,1)}), bf16[2,1,2,128,1024]{4,3,2,1,0:T(8,128)(2,1)S(1)}, u32[]{:S(2)}, u32[]{:S(2)}) async-start(bf16[2,1,2,128,1024]{4,3,2,1,0:T(8,128)(2,1)} %broadcast_in_dim.73), calls=%async_computation | async-start | bytes 2097152 | tf_op jit(solution)/shard_map/all_to_all | solution.py:11
  6.7 30.6 %copy-start.1 = (s32[2,27]{1,0:T(2,128)S(1)}, s32[2,27]{1,0:T(2,128)}, u32[]{:S(2)}) copy-start(s32[2,27]{1,0:T(2,128)} %param.6) | copy-start | bytes 652
  6.7 30.6 %copy-start.2 = (s32[2,27]{1,0:T(2,128)S(1)}, s32[2,27]{1,0:T(2,128)}, u32[]{:S(2)}) copy-start(s32[2,27]{1,0:T(2,128)} %param.7) | copy-start | bytes 652
  21.2 17.5 %all-to-all-start.1 = ((bf16[2,1,128,1024]{3,2,1,0:T(8,128)(2,1)}), bf16[2,1,128,1024]{3,2,1,0:T(8,128)(2,1)S(1)}, u32[]{:S(2)}, u32[]{:S(2)}) async-start(bf16[2,1,128,1024]{3,2,1,0:T(8,128)(2,1)} %pad_maximum_fusion), calls=%async_computation.1 | async-start | bytes 1048576 | tf_op jit(solution)/shard_map/all_to_all | solution.py:120
  24.8 31.8 %collective-permute-start.1 = (bf16[1,2,128,2048]{3,2,1,0:T(8,128)(2,1)S(1)}, bf16[1,2,128,2048]{3,2,1,0:T(8,128)(2,1)}, u32[]{:S(2)}, u32[]{:S(2)}) collective-permute-start(bf16[1,2,128,2048]{3,2,1,0:T(8,128)(2,1)S(1)} %bitcast.110), channel_id=1, source_target_pairs={{4,0},{8,4},{12,8},{16,12},{20,16},{24,20},{28,24},{32,28},{36,32}... | collective-permute-start | bytes 3145736 | tf_op jit(solution)/shard_map/ppermute | solution.py:39
  35.4 29.6 %collective-permute-start = (bf16[1,2,128,2048]{3,2,1,0:T(8,128)(2,1)S(1)}, bf16[1,2,128,2048]{3,2,1,0:T(8,128)(2,1)}, u32[]{:S(2)}, u32[]{:S(2)}) collective-permute-start(bf16[1,2,128,2048]{3,2,1,0:T(8,128)(2,1)S(1)} %bitcast.111), channel_id=1, source_target_pairs={{0,4},{4,8},{8,12},{12,16},{16,20},{20,24},{24,28},{28,32},{32,36}... | collective-permute-start | bytes 3145736 | tf_op jit(solution)/shard_map/ppermute | solution.py:37
  96.6 10.9 %all-to-all-start.3 = ((bf16[2,1,64,1024]{3,2,1,0:T(8,128)(2,1)}), bf16[2,1,64,1024]{3,2,1,0:T(8,128)(2,1)S(1)}, u32[]{:S(2)}, u32[]{:S(2)}) async-start(bf16[2,1,64,1024]{3,2,1,0:T(8,128)(2,1)} %copy.27), calls=%async_computation.3 | async-start | bytes 524288 | tf_op jit(solution)/shard_map/all_to_all | solution.py:62
